TPU v7x, 256 devices: a whole 4x4x8 slice. The times are simulated.
256 devices in a mesh: pop: 16 (over z_hi, x, core), shard: 16 (over y, z_lo).
Axes of the slice: x: 4, y: 4, z: 8 (z_hi: 2, z_lo: 4; z = z_hi * 4 + z_lo), core: 2. Of those that a mesh axis runs over, the one named last changes fastest.
Arguments:
- tokens: bfloat16 [32, 480, 4096], P('pop'), may hold values from -6 to 6
- gate_weight_matrix: bfloat16 [4096, 14336], P('pop', 'shard'), may hold values from -0.09375 to 0.09375
- w_up: bfloat16 [4096, 14336], P('pop', 'shard'), may hold values from -0.09375 to 0.09375
- a_gate: bfloat16 [32, 4, 4096], P('pop'), may hold values from -5 to 5
- a_up: bfloat16 [32, 4, 4096], P('pop'), may hold values from -5 to 5
- gate_hidden_factors: bfloat16 [32, 4, 14336], P('pop', None, 'shard'), may hold values from -5 to 5
- up_hidden_factors: bfloat16 [32, 4, 14336], P('pop', None, 'shard'), may hold values from -5 to 5
- fitness: bfloat16 [32], P('pop'), may hold values from -1 to 1
- readout: float32 [14336], P('shard'), may hold values from -0.13363062 to 0.13363062
Outputs:
- scores: float32 [32, 480], P('pop')
- upd_gate: float32 [4096, 14336], P('pop', 'shard')
- up_update_direction: float32 [4096, 14336], P('pop', 'shard')
All inputs are finite; a program needn't handle non-finite values.
Results may differ from a plain program's by a relative error of at most 0.0003.
Values may be sent and summed in bfloat16 or wider, within the bound.
A program may use at most 128 MiB of HBM per device.

v0:
```python
import math

import jax
import jax.numpy as jnp
from jax import lax
from jax.sharding import PartitionSpec as P


def direction(row_factor, col_factor, weighting):
    left_side = (row_factor.astype(jnp.float32) * weighting[:, None, None]).reshape(
        -1, row_factor.shape[2]
    )
    right_side = col_factor.astype(jnp.float32).reshape(-1, col_factor.shape[2])
    return lax.dot_general(
        left_side, right_side, (((0,), (0,)), ((), ())), precision=lax.Precision.HIGHEST
    )


def body(
    tokens,
    gate_weight_matrix,
    w_up,
    a_gate,
    a_up,
    gate_hidden_factors,
    up_hidden_factors,
    fitness,
    readout,
):
    members_dev, tok_count, model_width = tokens.shape
    row_count = members_dev * tok_count
    hidden_cols = gate_weight_matrix.shape[1]
    rank_count = a_gate.shape[1]
    noise_scale = 0.25 / math.sqrt(model_width * rank_count)
    flattened_rows = tokens.reshape(row_count, model_width)

    def add_rows(weight_rows):
        return jnp.dot(flattened_rows, weight_rows, preferred_element_type=jnp.float32)

    base_gate = add_rows(lax.all_gather(gate_weight_matrix, "pop", axis=0, tiled=True))
    base_up = add_rows(lax.all_gather(w_up, "pop", axis=0, tiled=True))
    gate_projected = jnp.einsum("mtd,mrd->mtr", tokens, a_gate, preferred_element_type=jnp.float32)
    up_projected = jnp.einsum("mtd,mrd->mtr", tokens, a_up, preferred_element_type=jnp.float32)
    noise_gate = jnp.einsum(
        "ygu,yup->ygp",
        gate_projected,
        gate_hidden_factors.astype(jnp.float32),
        precision=lax.Precision.HIGHEST,
    )
    noise_up = jnp.einsum(
        "ygu,yup->ygp",
        up_projected,
        up_hidden_factors.astype(jnp.float32),
        precision=lax.Precision.HIGHEST,
    )
    gate_pre = base_gate.reshape(members_dev, tok_count, hidden_cols) + noise_scale * noise_gate
    up_pre = base_up.reshape(members_dev, tok_count, hidden_cols) + noise_scale * noise_up
    hidden = jax.nn.silu(gate_pre) * up_pre
    partial_value = jnp.dot(
        hidden.reshape(row_count, hidden_cols), readout, precision=lax.Precision.HIGHEST
    ).reshape(members_dev, tok_count)
    scores = lax.psum(partial_value, "shard")
    col_gate, col_up, fitness_all = (
        lax.all_gather(gate_hidden_factors, "pop", axis=0, tiled=True),
        lax.all_gather(up_hidden_factors, "pop", axis=0, tiled=True),
        lax.all_gather(fitness, "pop", axis=0, tiled=True),
    )
    full_gate, full_up = (
        lax.all_gather(a_gate, "pop", axis=0, tiled=True),
        lax.all_gather(a_up, "pop", axis=0, tiled=True),
    )
    owned = model_width // lax.axis_size("pop")
    row_begin = lax.axis_index("pop") * owned
    row_gate = lax.dynamic_slice_in_dim(full_gate, row_begin, owned, 2)
    row_up = lax.dynamic_slice_in_dim(full_up, row_begin, owned, 2)
    total_members = fitness_all.shape[0]
    weighting = fitness_all.astype(jnp.float32) / math.sqrt(total_members * rank_count)
    upd_gate = direction(row_gate, col_gate, weighting)
    up_update_direction = direction(row_up, col_up, weighting)
    return (scores, upd_gate, up_update_direction)


def solution(mesh):
    placed = (
        P("pop", None, None),
        P("pop", "shard"),
        P("pop", "shard"),
        P("pop", None, None),
        P("pop", None, None),
        P("pop", None, "shard"),
        P("pop", None, "shard"),
        P("pop"),
        P("shard"),
    )
    return jax.shard_map(
        body,
        mesh=mesh,
        in_specs=placed,
        out_specs=(P("pop", None), P("pop", "shard"), P("pop", "shard")),
        check_vma=False,
    )
```

profile of v0, /device:TPU:1, one launch (start us, length us, event | category | flops | bytes accessed | tf_op | source)
XLA Modules:
  0.0 377.9 jit_solution(7362858366357543477)
XLA Ops:
  7.2 0.0 all-gather.9.cloned.1.call-start
  7.2 0.7 all-gather.9.cloned.1.call-update
  7.9 0.0 all-gather.11.cloned.1.call-start
  7.9 0.7 all-gather.11.cloned.1.call-update
  8.6 0.0 all-gather.5.cloned.1.call-start
  8.7 0.7 all-gather.5.cloned.1.call-update
  9.4 0.0 all-gather.7.cloned.1.call-start
  9.4 0.5 all-gather.7.cloned.1.call-update
  10.0 0.7 reshape.29
  10.7 1.3 dynamic-slice
  12.6 0.9 dynamic-update-slice
  13.4 46.0 %all-reduce = bf16[32]{0:T(256)(128)(2,1)S(1)} all-reduce(bf16[32]{0:T(256)(128)(2,1)S(1)} %dynamic-update-slice), channel_id=1, replica_groups=mesh['pop'=16,'shard'=16] {'pop'}, use_global_device_ids=true, to_apply=%add | all-reduce | flops 32 | bytes 128
  59.5 34.2 %all_gather.25 = bf16[32,4,896]{2,1,0:T(4,128)(2,1)} all-gather(bf16[2,4,896]{2,1,0:T(4,128)(2,1)} %param.14), channel_id=1, replica_groups=mesh['pop'=16,'shard'=16] {'pop'}, dimensions={0}, use_global_device_ids=true | all-gather | bytes 243712 | tf_op jit(solution)/shard_map/all_gather | solution.py:64
  93.7 28.0 %all_gather.27 = bf16[32,4,896]{2,1,0:T(4,128)(2,1)} all-gather(bf16[2,4,896]{2,1,0:T(4,128)(2,1)} %param.15), channel_id=1, replica_groups=mesh['pop'=16,'shard'=16] {'pop'}, dimensions={0}, use_global_device_ids=true | all-gather | bytes 243712 | tf_op jit(solution)/shard_map/all_gather | solution.py:65
  121.7 5.5 %fusion.31 = f32[2,480,4]{1,2,0:T(4,128)S(1)} fusion(bf16[2,480,4096]{2,1,0:T(8,128)(2,1)} %param.9, bf16[2,4,4096]{2,1,0:T(4,128)(2,1)} %param.13), kind=kOutput, calls=%fused_computation.37 | convolution fusion | flops 31457280 | bytes 7945216 | tf_op jit(solution)/shard_map/mtd,mrd->mtr/dot_general | solution.py:43
  127.2 0.0 copy-done.3
  127.2 1.8 fusion.32
  129.1 0.0 copy-done
  129.1 0.0 copy-start.4
  129.1 2.1 fusion.29
  131.2 3.6 fusion.30
  134.8 0.9 constant_dynamic-slice_fusion.1
  135.7 0.0 all-gather.11.cloned.1.call-done
  135.7 0.9 constant_dynamic-slice_fusion
  136.6 2.5 convolution_bitcast_fusion
  139.1 2.5 convolution_bitcast_fusion.1
  141.6 83.4 %all-gather.5.cloned.1.call-done = bf16[4096,896]{1,0:T(8,128)(2,1)} async-done(((bf16[256,896]{1,0:T(8,128)(2,1)}), bf16[4096,896]{1,0:T(8,128)(2,1)}) %all-gather.5.cloned.1.call-update) | async-done | bytes 7340048 | tf_op jit(solution)/shard_map/all_gather | solution.py:40
  225.0 13.9 %fusion.2 = f32[2,480,896]{2,1,0:T(8,128)} fusion(bf16[2,480,4096]{2,1,0:T(8,128)(2,1)} %param.9, bf16[4096,896]{1,0:T(8,128)(2,1)} %all-gather.5.cloned.1.call-done), kind=kOutput, calls=%fused_computation.2 | convolution fusion | flops 7046430720 | bytes 18644992 | tf_op jit(solution)/shard_map/dot_general | solution.py:38
  238.9 83.8 %all-gather.7.cloned.1.call-done = bf16[4096,896]{1,0:T(8,128)(2,1)} async-done(((bf16[256,896]{1,0:T(8,128)(2,1)}), bf16[4096,896]{1,0:T(8,128)(2,1)}) %all-gather.7.cloned.1.call-update) | async-done | bytes 7340048 | tf_op jit(solution)/shard_map/all_gather | solution.py:41
  322.8 11.9 %fusion = f32[2,480,896]{2,1,0:T(8,128)S(1)} fusion(bf16[2,480,4096]{2,1,0:T(8,128)(2,1)} %param.9, bf16[4096,896]{1,0:T(8,128)(2,1)} %all-gather.7.cloned.1.call-done), kind=kOutput, calls=%fused_computation | convolution fusion | flops 7046430720 | bytes 18644992 | tf_op jit(solution)/shard_map/dot_general | solution.py:38
  334.7 4.3 %fusion.4 = f32[1,2,480]{2,0,1:T(1,128)S(1)} fusion(f32[896,1,1]{0,1,2:T(1,128)S(1)} %reshape.29, f32[2,480,896]{2,1,0:T(8,128)S(1)} %fusion, f32[2,480,896]{2,1,0:T(8,128)S(1)} %fusion.32, f32[2,480,896]{2,1,0:T(8,128)S(1)} %copy-done.5, f32[2,480,896]{2,1,0:T(8,128)S(1)} %copy-done.1), kind=kOutput, calls=%fused_computation.4 | convolution fusion | flops 18063360 | bytes 13769984 | tf_op jit(solution)/shard_map/dot_general | solution.py:59
  338.9 32.5 %psum.7 = f32[2,480]{1,0:T(2,128)} all-reduce(f32[2,480]{1,0:T(2,128)S(1)} %bitcast.25), channel_id=1, replica_groups=mesh['pop'=16,'shard'=16] {'shard'}, use_global_device_ids=true, to_apply=%region_0.1 | all-reduce | flops 960 | bytes 7680 | tf_op jit(solution)/shard_map/psum | solution.py:62
  (13 shorter events, 0.0 us)
Async XLA Ops:
  7.2 127.6 %all-gather.9.cloned.1.call-start = ((), (), s32[]{:S(2)}) async-start(), calls=%async_computation.2 | async-start | bytes 1114112 | tf_op jit(solution)/shard_map/all_gather | solution.py:69
  7.9 127.8 %all-gather.11.cloned.1.call-start = ((), (), s32[]{:S(2)}) async-start(), calls=%async_computation.3 | async-start | bytes 1114112 | tf_op jit(solution)/shard_map/all_gather | solution.py:70
  8.6 216.3 %all-gather.5.cloned.1.call-start = ((), (), s32[]{:S(2)}) async-start(), calls=%async_computation | async-start | bytes 7798784 | tf_op jit(solution)/shard_map/all_gather | solution.py:40
  9.4 313.4 %all-gather.7.cloned.1.call-start = ((), (), s32[]{:S(2)}) async-start(), calls=%async_computation.1 | async-start | bytes 7798784 | tf_op jit(solution)/shard_map/all_gather | solution.py:41
  121.7 5.5 %copy-start.3 = (bf16[2,4,896]{2,1,0:T(4,128)(2,1)S(1)}, bf16[2,4,896]{2,1,0:T(4,128)(2,1)}, u32[]{:S(2)}) copy-start(bf16[2,4,896]{2,1,0:T(4,128)(2,1)} %param.15) | copy-start | bytes 43012
  121.7 7.4 %copy-start = (bf16[2,480,4096]{2,1,0:T(8,128)(2,1)S(1)}, bf16[2,480,4096]{2,1,0:T(8,128)(2,1)}, u32[]{:S(2)}) copy-start(bf16[2,480,4096]{2,1,0:T(8,128)(2,1)} %param.9) | copy-start | bytes 23592964
  127.2 1.9 copy-start.2
  129.1 2.1 copy-start.4
  322.8 11.9 %copy-start.1 = (f32[2,480,896]{2,1,0:T(8,128)S(1)}, f32[2,480,896]{2,1,0:T(8,128)}, u32[]{:S(2)}) copy-start(f32[2,480,896]{2,1,0:T(8,128)} %fusion.30) | copy-start | bytes 10321924
  322.8 11.9 %copy-start.5 = (f32[2,480,896]{2,1,0:T(8,128)S(1)}, f32[2,480,896]{2,1,0:T(8,128)}, u32[]{:S(2)}) copy-start(f32[2,480,896]{2,1,0:T(8,128)} %fusion.2) | copy-start | bytes 10321924
Sparse Core Ops, SparseCore 0:
  10.7 59.8 all-gather.8
  73.4 51.5 all-gather.10
  127.7 97.2 all-gather.4
  227.6 95.1 all-gather.6
where the time goes:
time: 383 us; the launch traced here: 378 us
  waiting for transfers between devices  170 us (44%)
  blocking collectives  141 us (37%)
  matrix products  48.1 us (13%)
  between operations  14.5 us (4%)
  local copies, waits for them, and re-layouts  4.59 us (1%)
    all_gather x1, waiting for transfers between devices, body(): base_up = add_rows(lax.all_gather(w_up, 'pop', axis=0, tiled=True))  83.8 us
    all_gather x1, waiting for transfers between devices, body(): lax.all_gather(gate_weight_matrix, 'pop', axis=0, tiled=True)  83.4 us
    unnamed x1, blocking collectives  46 us
    all_gather x1, blocking collectives, body(): lax.all_gather(gate_hidden_factors, 'pop', axis=0, tiled=True)  34.2 us
    psum x1, blocking collectives, body(): scores = lax.psum(partial_value, 'shard')  32.5 us
    all_gather x1, blocking collectives, body(): lax.all_gather(up_hidden_factors, 'pop', axis=0, tiled=True)  28 us
    dot_general x2, matrix products, add_rows(): jnp.dot(flattened_rows, weight_rows, preferred_element_type=jnp.float32)  25.8 us
  transfers between devices with their start and end apart: 4, of which 2 were waited for; matrix products, arithmetic and copies ran while one was open for 10% of the time, Pallas kernels for 0%

commit v1 on v0

v1 whole, which is shorter than its diff:
```python
import functools
import math

import jax
import jax.numpy as jnp
from jax import lax
from jax.experimental import pallas as pl
from jax.experimental.pallas import tpu as pltpu
from jax.sharding import PartitionSpec as P

MESH = pl.DeviceIdType.MESH
F32 = jnp.float32
BF16 = jnp.bfloat16
LANES = 128
RING = 4
CORES = 2
SMALL = 16
(Z, A_LO, A_HI, B_LO, B_HI, RA_LO, RA_HI, RB_LO, RB_HI,
 S_OWN, S_Z, S_A_LO, S_A_HI, S_B_LO, S_B_HI, S_RA, S_RB) = range(17)
KINDS = 17


def dot(a, b, dims=((1,), (0,)), precision=None):
    return lax.dot_general(a, b, (dims, ((), ())), precision=precision, preferred_element_type=F32)


def kernel(
    noise, out_scale, n_pop, n_shard,
    tok_hbm, wg_hbm, wu_hbm, ag_hbm, au_hbm, hg_hbm, hu_hbm, fit_ref, ro_ref,
    sc_ref, ug_hbm, uu_hbm,
    tok, gath, acc, total, ext, fac, ag, au, hg, hu, msg, abuf, left, stage, parts,
    send, recv, wsem, lsem, asend, arecv, bsend, brecv, psend, precv, osem,
):
    pop, sh = lax.axis_index("pop"), lax.axis_index("shard")
    core, chip = pop % CORES, pop // CORES
    x, zh = chip % RING, chip // RING
    chunks = gath.shape[0]
    depth = wg_hbm.shape[0]
    rows = tok.shape[0]
    members = tok_hbm.shape[0]
    per_member = rows // members
    block = 2 * depth + SMALL
    first = depth + SMALL
    span = CORES * depth

    def at(dx, dz):
        return (zh + dz) % 2 * RING + (x + dx) % RING

    def dev(c, k):
        return (c * CORES + k, sh)

    own, zown = at(0, 0), at(0, 1)
    xp, xm, xx = at(1, 0), at(3, 0), at(2, 0)
    zp, zm, zx = at(1, 1), at(3, 1), at(2, 1)

    barrier = pltpu.get_barrier_semaphore()

    @pl.loop(1, n_pop)
    def _(d):
        pl.semaphore_signal(barrier, inc=1, device_id=((pop + d) % n_pop, sh), device_id_type=MESH)

    @pl.loop(1, n_shard)
    def _(d):
        pl.semaphore_signal(barrier, inc=1, device_id=(pop, (sh + d) % n_shard), device_id_type=MESH)

    def weight_load(t, k):
        src = (wg_hbm, wu_hbm)[k]
        col = pl.multiple_of(t * LANES, LANES)
        return pltpu.make_async_copy(
            src.at[:, pl.ds(col, LANES)], gath.at[t, own, core, pl.ds(k * depth, depth)], wsem.at[k, t]
        )

    small_loads = [
        pltpu.make_async_copy(a, b, lsem.at[i])
        for i, (a, b) in enumerate(((hg_hbm, hg), (hu_hbm, hu), (ag_hbm, ag), (au_hbm, au)))
    ]
    tok_loads = [
        pltpu.make_async_copy(
            tok_hbm.at[m], tok.at[pl.ds(m * per_member, per_member)], lsem.at[4 + m]
        )
        for m in range(members)
    ]
    for c in small_loads:
        c.start()

    @pl.loop(0, chunks)
    def _(t):
        weight_load(t, 0).start()
        weight_load(t, 1).start()

    for c in tok_loads:
        c.start()

    for c in small_loads[:2]:
        c.wait()

    def pack(gate, up):
        return jnp.concatenate(
            [gate[0].astype(F32), gate[1].astype(F32), up[0].astype(F32), up[1].astype(F32)], axis=0
        ).astype(BF16)

    factors = pack(hg, hu)
    for t in range(chunks):
        gath[t, own, core, 2 * depth:, :] = factors[:, t * LANES:(t + 1) * LANES]

    @pl.loop(0, chunks)
    def _(t):
        weight_load(t, 0).wait()
        weight_load(t, 1).wait()

    pl.semaphore_wait(barrier, n_pop - 1 + n_shard - 1)

    def remote(kind, t, c, k, target, lo=0, n=block):
        ref = gath.at[t, c, k, pl.ds(lo, n)]
        return pltpu.make_async_remote_copy(
            src_ref=ref, dst_ref=ref, send_sem=send.at[kind, t], recv_sem=recv.at[kind, t],
            device_id=target, device_id_type=MESH,
        )

    to_z, to_p, to_m, to_s = dev(zown, core), dev(xp, core), dev(xm, core), dev(own, 1 - core)
    second = block - first

    sends = {
        Z: (own, 0, block, to_z),
        A_LO: (own, 0, block, to_p), A_HI: (own, 0, block, to_m),
        B_LO: (zown, 0, block, to_p), B_HI: (zown, 0, block, to_m),
        RA_LO: (xm, 0, first, to_p), RA_HI: (xp, first, second, to_m),
        RB_LO: (zm, first, second, to_p), RB_HI: (zp, 0, first, to_m),
        S_OWN: (own, 0, block, to_s), S_Z: (zown, 0, block, to_s),
        S_A_LO: (xm, 0, block, to_s), S_A_HI: (xp, 0, block, to_s),
        S_B_LO: (zm, 0, block, to_s), S_B_HI: (zp, 0, block, to_s),
        S_RA: (xx, 0, block, to_s), S_RB: (zx, 0, block, to_s),
    }
    arrives = {
        Z: (zown, core, 0, block),
        A_LO: (xm, core, 0, block), A_HI: (xp, core, 0, block),
        B_LO: (zm, core, 0, block), B_HI: (zp, core, 0, block),
        RA_LO: (xx, core, 0, first), RA_HI: (xx, core, first, second),
        RB_LO: (zx, core, first, second), RB_HI: (zx, core, 0, first),
    }
    for kind in range(S_OWN, KINDS):
        arrives[kind] = (sends[kind][0], 1 - core, 0, block)

    def put(kind, t):
        c, lo, n, target = sends[kind]
        remote(kind, t, c, core, target, lo, n).start()

    def got(kind, t):
        c, k, lo, n = arrives[kind]
        remote(kind, t, c, k, to_s, lo, n).wait_recv()

    put(Z, 0)

    for c in small_loads[2:]:
        c.wait()
    rank_rows = pack(ag, au)
    for k in range(3):
        fac[k * SMALL:(k + 1) * SMALL, :] = rank_rows
    fac[3 * SMALL:, :] = jnp.zeros((LANES - 3 * SMALL, fac.shape[1]), BF16)
    fit = fit_ref[...].astype(F32)
    row16 = lax.broadcasted_iota(jnp.int32, (SMALL, LANES), 0)
    f0 = jnp.broadcast_to(fit[:, 0:1], (SMALL, LANES))
    f1 = jnp.broadcast_to(fit[:, 1:2], (SMALL, LANES))
    fit_rows = jnp.where(row16 // 4 % 2 == 0, f0, f1).astype(BF16)
    for q in range(n_pop):
        msg[q, :, :depth] = rank_rows[:, q * depth:(q + 1) * depth]
        msg[q, :, depth:] = fit_rows

    def factor_copy(q):
        return pltpu.make_async_remote_copy(
            src_ref=msg.at[q], dst_ref=abuf.at[sh], send_sem=asend.at[q], recv_sem=arecv.at[0],
            device_id=(q, sh), device_id_type=MESH,
        )

    def spread_copy(s, target):
        return pltpu.make_async_remote_copy(
            src_ref=abuf.at[s], dst_ref=abuf.at[s], send_sem=bsend.at[target], recv_sem=brecv.at[s],
            device_id=(pop, target), device_id_type=MESH,
        )

    @pl.when(pop == sh)
    def _():
        @pl.loop(1, n_pop)
        def _(d):
            factor_copy((pop + d) % n_pop).start()
        abuf[pop] = msg[pop]

    total[...] = jnp.zeros_like(total)

    def project():
        for c in tok_loads:
            c.wait()
        acc[0, :, :LANES] = jnp.zeros((rows, LANES), F32)

        @pl.loop(0, tok.shape[1] // span)
        def _(k):
            cols = pl.ds(pl.multiple_of(k * span, span), span)
            acc[0, :, :LANES] += dot(tok[:, cols], fac[:, cols], ((1,), (1,)))

        row = lax.broadcasted_iota(jnp.int32, (rows, LANES), 0)
        lane = lax.broadcasted_iota(jnp.int32, (rows, LANES), 1)
        mine = (row // per_member) == (lane // 4 % 2)
        p = jnp.where(mine, acc[0, :, :LANES] * noise, 0.0)
        hi = p.astype(BF16).astype(F32)
        mid = (p - hi).astype(BF16).astype(F32)
        lo = p - hi - mid
        group = lane // SMALL
        ext[...] = jnp.where(group == 0, hi, jnp.where(group == 1, mid, lo)).astype(BF16)

    def split_rows(v):
        n = v.shape[0]
        gate_row = lax.broadcasted_iota(jnp.int32, (n, LANES), 0) % SMALL < SMALL // 2
        vf = v.astype(F32)
        return jnp.concatenate(
            [jnp.where(gate_row, vf, 0.0), jnp.where(gate_row, 0.0, vf)], axis=1
        ).astype(BF16)

    def start_chunk(t, slot):
        rhs = split_rows(gath[t, own, core, 2 * depth:, :])
        pad = jnp.zeros((LANES - 3 * SMALL, 2 * LANES), BF16)
        acc[slot] = dot(ext[...], jnp.concatenate([rhs, rhs, rhs, pad], axis=0))

    def add_chip(t, slot, c):
        cols = pl.ds(pl.multiple_of(c * span, span), span)
        gate = gath[t, c, :, :depth, :].reshape(span, LANES)
        up = gath[t, c, :, depth:2 * depth, :].reshape(span, LANES)
        acc[slot] += dot(tok[:, cols], jnp.concatenate([gate, up], axis=1))

    def finish_chunk(t, slot):
        gate, up = acc[slot, :, :LANES], acc[slot, :, LANES:]
        hidden = gate / (1.0 + jnp.exp(-gate)) * up
        total[...] += hidden * ro_ref[pl.ds(t, 1), :]

    def build_left():
        a = abuf[:, :, :depth].reshape(n_pop * SMALL, depth).astype(F32)
        f = abuf[:, :, depth:].reshape(n_pop * SMALL, LANES).astype(F32)
        prod = (a * jnp.concatenate([f] * (depth // LANES), axis=1)).T
        hi = prod.astype(BF16)
        left[:, :n_pop * SMALL] = hi
        left[:, n_pop * SMALL:] = (prod - hi.astype(F32)).astype(BF16)

    def out_copy(t, k):
        dst = (ug_hbm, uu_hbm)[k]
        col = pl.multiple_of(t * LANES, LANES)
        return pltpu.make_async_copy(stage.at[t, k], dst.at[:, pl.ds(col, LANES)], osem.at[k, t])

    def update_chunk(t):
        right = split_rows(gath[t, :, :, 2 * depth:, :].reshape(n_pop * SMALL, LANES))
        upd = dot(left[...], jnp.concatenate([right, right], axis=0)) * out_scale
        stage[t, 0] = upd[:, :LANES]
        stage[t, 1] = upd[:, LANES:]
        out_copy(t, 0).start()
        out_copy(t, 1).start()

    def phase_two(t, slot):
        got(S_RA, t)
        add_chip(t, slot, xx)
        got(S_RB, t)
        add_chip(t, slot, zx)
        finish_chunk(t, slot)

    @pl.loop(0, chunks + 2)
    def _(i):
        @pl.when(i < chunks)
        def _():
            put(A_LO, i)
            put(A_HI, i)

            @pl.when(i + 1 < chunks)
            def _():
                put(Z, i + 1)
            put(S_OWN, i)
            got(Z, i)
            put(B_LO, i)
            put(B_HI, i)
            put(S_Z, i)

        @pl.when((i >= 1) & (i < chunks + 1))
        def _():
            t = i - 1
            for kind, relay, copy in (
                (A_LO, RA_LO, S_A_LO), (A_HI, RA_HI, S_A_HI),
                (B_LO, RB_LO, S_B_LO), (B_HI, RB_HI, S_B_HI),
            ):
                got(kind, t)
                put(relay, t)
                put(copy, t)

        @pl.when(i >= 2)
        def _():
            t = i - 2
            got(RA_LO, t)
            got(RA_HI, t)
            put(S_RA, t)
            got(RB_LO, t)
            got(RB_HI, t)
            put(S_RB, t)

        @pl.when(i == 0)
        def _():
            project()

        @pl.when(i == 1)
        def _():
            @pl.when(pop != sh)
            def _():
                factor_copy(pop).wait_recv()

            @pl.loop(1, n_shard)
            def _(d):
                spread_copy(sh, (sh + d) % n_shard).start()

        @pl.when((i >= 1) & (i < chunks + 1))
        def _():
            t = i - 1
            for kind in (S_OWN, S_Z, S_A_LO, S_A_HI, S_B_LO, S_B_HI):
                got(kind, t)
            start_chunk(t, t % 2)

            @pl.loop(0, 6)
            def _(j):
                q = j // 2
                add_chip(t, t % 2, at(q + q // 2, j % 2))

        @pl.when(i >= 2)
        def _():
            phase_two(i - 2, i % 2)

        @pl.when(i == 2)
        def _():
            @pl.loop(1, n_shard)
            def _(d):
                spread_copy((sh + d) % n_shard, sh).wait_recv()
            build_left()

        @pl.when((i >= 2) & (i < chunks + 1))
        def _():
            update_chunk(i - 2)

    ones = jnp.ones((8, LANES), F32)
    for m in range(members):
        part = dot(ones, total[m * per_member:(m + 1) * per_member, :], ((1,), (1,)), lax.Precision.HIGHEST)
        parts[sh, m:m + 1, :] = part[0:1, :]

    def score_copy(s, target):
        return pltpu.make_async_remote_copy(
            src_ref=parts.at[s], dst_ref=parts.at[s], send_sem=psend.at[target], recv_sem=precv.at[s],
            device_id=(pop, target), device_id_type=MESH,
        )

    @pl.loop(1, n_shard)
    def _(d):
        score_copy(sh, (sh + d) % n_shard).start()

    update_chunk(chunks - 1)

    @pl.loop(0, chunks)
    def _(t):
        for kind in range(KINDS):
            c, lo, n, target = sends[kind]
            remote(kind, t, c, core, target, lo, n).wait_send()

    @pl.when(pop == sh)
    def _():
        @pl.loop(1, n_pop)
        def _(d):
            factor_copy((pop + d) % n_pop).wait_send()

    @pl.loop(1, n_shard)
    def _(d):
        spread_copy(sh, (sh + d) % n_shard).wait_send()
        score_copy(sh, (sh + d) % n_shard).wait_send()

    @pl.loop(1, n_shard)
    def _(d):
        score_copy((sh + d) % n_shard, sh).wait_recv()

    score = parts[0]
    for s in range(1, n_shard):
        score = score + parts[s]
    sc_ref[...] = score

    @pl.loop(0, chunks)
    def _(t):
        out_copy(t, 0).wait()
        out_copy(t, 1).wait()


def body(n_pop, n_shard, tokens, wg, wu, a_gate, a_up, h_gate, h_up, fitness, readout):
    members, tok_count, width = tokens.shape
    depth, cols = wg.shape
    ranks = a_gate.shape[1]
    chunks = cols // LANES
    rows = members * tok_count
    chips = n_pop // CORES
    noise = 0.25 / math.sqrt(width * ranks)
    out_scale = 1.0 / math.sqrt(n_pop * members * ranks)
    block = 2 * depth + SMALL
    dma = pltpu.SemaphoreType.DMA
    anyspec = pl.BlockSpec(memory_space=pl.ANY)
    vspec = pl.BlockSpec(memory_space=pltpu.VMEM)
    return pl.pallas_call(
        functools.partial(kernel, noise, out_scale, n_pop, n_shard),
        name="generation",
        out_shape=(
            jax.ShapeDtypeStruct((members, tok_count), F32),
            jax.ShapeDtypeStruct((depth, cols), F32),
            jax.ShapeDtypeStruct((depth, cols), F32),
        ),
        in_specs=[anyspec] * 7 + [vspec, vspec],
        out_specs=(vspec, anyspec, anyspec),
        scratch_shapes=[
            pltpu.VMEM((rows, width), BF16),
            pltpu.VMEM((chunks, chips, CORES, block, LANES), BF16),
            pltpu.VMEM((2, rows, 2 * LANES), F32),
            pltpu.VMEM((rows, LANES), F32),
            pltpu.VMEM((rows, LANES), BF16),
            pltpu.VMEM((LANES, width), BF16),
            pltpu.VMEM((members, ranks, width), BF16),
            pltpu.VMEM((members, ranks, width), BF16),
            pltpu.VMEM((members, ranks, cols), BF16),
            pltpu.VMEM((members, ranks, cols), BF16),
            pltpu.VMEM((n_pop, SMALL, depth + LANES), BF16),
            pltpu.VMEM((n_pop, SMALL, depth + LANES), BF16),
            pltpu.VMEM((depth, 2 * n_pop * SMALL), BF16),
            pltpu.VMEM((chunks, 2, depth, LANES), F32),
            pltpu.VMEM((n_shard, members, tok_count), F32),
            dma((KINDS, chunks)), dma((KINDS, chunks)),
            dma((2, chunks)), dma((6,)),
            dma((n_pop,)), dma((1,)),
            dma((n_shard,)), dma((n_shard,)),
            dma((n_shard,)), dma((n_shard,)),
            dma((2, chunks)),
        ],
        compiler_params=pltpu.CompilerParams(
            collective_id=0, has_side_effects=True, vmem_limit_bytes=56 * 1024 * 1024
        ),
    )(tokens, wg, wu, a_gate, a_up, h_gate, h_up, fitness.reshape(1, members), readout.reshape(chunks, LANES))


def solution(mesh):
    placed = (
        P("pop", None, None),
        P("pop", "shard"),
        P("pop", "shard"),
        P("pop", None, None),
        P("pop", None, None),
        P("pop", None, "shard"),
        P("pop", None, "shard"),
        P("pop"),
        P("shard"),
    )
    return jax.shard_map(
        functools.partial(body, mesh.shape["pop"], mesh.shape["shard"]),
        mesh=mesh,
        in_specs=placed,
        out_specs=(P("pop", None), P("pop", "shard"), P("pop", "shard")),
        check_vma=False,
    )
```

time: 383 us -> 105 us (0.27)
  waiting for transfers between devices: 170 us -> 0 us
  blocking collectives: 141 us -> 0 us
  Pallas kernels: 0 us -> 97.1 us
  matrix products: 48.1 us -> 0 us
  between operations: 14.5 us -> 0.64 us
    all_gather x4 -> x0, waiting for transfers between devices: 167 us -> none  [the longest x1 83.8 us: body(): base_up = add_rows(lax.all_gather(w_up, 'pop', axis=0, tiled=True))]
    pallas_call x0 -> x1, Pallas kernels: none -> 97.1 us  [body(): pl.pallas_call(functools.partial(kernel, noise, out_scale, n_pop, n_shard...]
    all_gather x2 -> x0, blocking collectives: 62.2 us -> none  [the longest x1 34.2 us: body(): lax.all_gather(gate_hidden_factors, 'pop', axis=0, tiled=True)]
    dot_general x9 -> x0, matrix products: 48.1 us -> none  [the longest x2 25.8 us: add_rows(): jnp.dot(flattened_rows, weight_rows, preferred_element_type=jnp.float32)]
    unnamed x1 -> x0, blocking collectives: 46 us -> none
    psum x1 -> x0, blocking collectives: 32.5 us -> none  [body(): scores = lax.psum(partial_value, 'shard')]
  transfers between devices with their start and end apart: 4 -> 0, of which waited for: 2 -> 0; matrix products, arithmetic and copies ran while one was open for 10% -> 0% of each run, Pallas kernels for 0% -> 0%
where the time goes in v1:
time: 105 us; the launch traced here: 103 us
  Pallas kernels  97.1 us (92%)
  local copies, waits for them, and re-layouts  5.58 us (5%)
    pallas_call x1, Pallas kernels, body(): pl.pallas_call(functools.partial(kernel, noise, out_scale, n_pop, n_shard...  97.1 us
    unnamed x3, local copies, waits for them, and re-layouts  5.58 us

profile of v1, /device:TPU:1, one launch (start us, length us, event | category | flops | bytes accessed | tf_op | source)
XLA Modules:
  0.0 103.3 jit_solution(13779855489434231053)
XLA Ops:
  0.6 97.1 %generation.1 = (f32[2,480]{1,0:T(2,128)}, f32[256,896]{1,0:T(8,128)}, f32[256,896]{1,0:T(8,128)}) custom-call(bf16[2,480,4096]{2,1,0:T(8,128)(2,1)} %tok_hbm.1, bf16[256,896]{1,0:T(8,128)(2,1)} %wg_hbm.1, bf16[256,896]{1,0:T(8,128)(2,1)} %wu_hbm.1, bf16[2,4,4096]{2,1,0:T(4,128)(2,1)} %ag_hbm.1, bf16[2,4,4096]{2,1,0:T(4,128)(2,1)} %au_hbm.1, ...), custom_call_target="tpu_custom_call" | custom-call | tf_op jit(solution)/shard_map/generation/pallas_call | solution.py:402
  97.7 1.3 %copy.15 = f32[2,480]{1,0:T(2,128)} copy(f32[2,480]{1,0:T(2,128)} %get-tuple-element.6) | data formatting | bytes 7680
  99.0 2.2 %copy.16 = f32[256,896]{1,0:T(8,128)} copy(f32[256,896]{1,0:T(8,128)} %get-tuple-element.7) | data formatting | bytes 1835008
  101.2 2.2 %copy.17 = f32[256,896]{1,0:T(8,128)} copy(f32[256,896]{1,0:T(8,128)} %get-tuple-element.8) | data formatting | bytes 1835008

commit v2 on v1

--- a/solution.py
+++ b/solution.py
@@ -15,20 +15,29 @@
 RING = 4
 CORES = 2
 SMALL = 16
-(Z, A_LO, A_HI, B_LO, B_HI, RA_LO, RA_HI, RB_LO, RB_HI,
- S_OWN, S_Z, S_A_LO, S_A_HI, S_B_LO, S_B_HI, S_RA, S_RB) = range(17)
-KINDS = 17
+(Z, ZX, A_LO, A_HI, B_LO, B_HI, RA_LO, RA_HI, RB_LO, RB_HI,
+ S_OWN, S_Z, S_A_LO, S_A_HI, S_B_LO, S_B_HI, S_RA, S_RB) = range(18)
+KINDS = 18
 
 
 def dot(a, b, dims=((1,), (0,)), precision=None):
     return lax.dot_general(a, b, (dims, ((), ())), precision=precision, preferred_element_type=F32)
 
 
+def split_rows(v):
+    n = v.shape[0]
+    gate_row = lax.broadcasted_iota(jnp.int32, (n, LANES), 0) % SMALL < SMALL // 2
+    vf = v.astype(F32)
+    return jnp.concatenate(
+        [jnp.where(gate_row, vf, 0.0), jnp.where(gate_row, 0.0, vf)], axis=1
+    ).astype(BF16)
+
+
 def kernel(
-    noise, out_scale, n_pop, n_shard,
-    tok_hbm, wg_hbm, wu_hbm, ag_hbm, au_hbm, hg_hbm, hu_hbm, fit_ref, ro_ref,
-    sc_ref, ug_hbm, uu_hbm,
-    tok, gath, acc, total, ext, fac, ag, au, hg, hu, msg, abuf, left, stage, parts,
+    noise, n_pop, n_shard,
+    tok_hbm, wg_hbm, wu_hbm, ag_hbm, au_hbm, hg_hbm, hu_hbm, fit_hbm, ro_hbm,
+    sc_ref, left, right_hbm,
+    tok, gath, acc, total, ext, fac, ag, au, hg, hu, fit_ref, ro_ref, msg, abuf, parts,
     send, recv, wsem, lsem, asend, arecv, bsend, brecv, psend, precv, osem,
 ):
     pop, sh = lax.axis_index("pop"), lax.axis_index("shard")
@@ -53,16 +62,6 @@
     xp, xm, xx = at(1, 0), at(3, 0), at(2, 0)
     zp, zm, zx = at(1, 1), at(3, 1), at(2, 1)
 
-    barrier = pltpu.get_barrier_semaphore()
-
-    @pl.loop(1, n_pop)
-    def _(d):
-        pl.semaphore_signal(barrier, inc=1, device_id=((pop + d) % n_pop, sh), device_id_type=MESH)
-
-    @pl.loop(1, n_shard)
-    def _(d):
-        pl.semaphore_signal(barrier, inc=1, device_id=(pop, (sh + d) % n_shard), device_id_type=MESH)
-
     def weight_load(t, k):
         src = (wg_hbm, wu_hbm)[k]
         col = pl.multiple_of(t * LANES, LANES)
@@ -72,15 +71,15 @@
 
     small_loads = [
         pltpu.make_async_copy(a, b, lsem.at[i])
-        for i, (a, b) in enumerate(((hg_hbm, hg), (hu_hbm, hu), (ag_hbm, ag), (au_hbm, au)))
+        for i, (a, b) in enumerate(((hg_hbm, hg), (hu_hbm, hu), (ag_hbm, ag), (au_hbm, au), (fit_hbm, fit_ref), (ro_hbm, ro_ref)))
     ]
     tok_loads = [
         pltpu.make_async_copy(
-            tok_hbm.at[m], tok.at[pl.ds(m * per_member, per_member)], lsem.at[4 + m]
+            tok_hbm.at[m], tok.at[pl.ds(m * per_member, per_member)], lsem.at[6 + m]
         )
         for m in range(members)
     ]
-    for c in small_loads:
+    for c in small_loads[:2]:
         c.start()
 
     @pl.loop(0, chunks)
@@ -88,8 +87,18 @@
         weight_load(t, 0).start()
         weight_load(t, 1).start()
 
-    for c in tok_loads:
+    for c in small_loads[2:] + tok_loads:
         c.start()
+
+    barrier = pltpu.get_barrier_semaphore()
+
+    @pl.loop(1, n_pop)
+    def _(d):
+        pl.semaphore_signal(barrier, inc=1, device_id=((pop + d) % n_pop, sh), device_id_type=MESH)
+
+    @pl.loop(1, n_shard)
+    def _(d):
+        pl.semaphore_signal(barrier, inc=1, device_id=(pop, (sh + d) % n_shard), device_id_type=MESH)
 
     for c in small_loads[:2]:
         c.wait()
@@ -102,11 +111,6 @@
     factors = pack(hg, hu)
     for t in range(chunks):
         gath[t, own, core, 2 * depth:, :] = factors[:, t * LANES:(t + 1) * LANES]
-
-    @pl.loop(0, chunks)
-    def _(t):
-        weight_load(t, 0).wait()
-        weight_load(t, 1).wait()
 
     pl.semaphore_wait(barrier, n_pop - 1 + n_shard - 1)
 
@@ -121,7 +125,7 @@
     second = block - first
 
     sends = {
-        Z: (own, 0, block, to_z),
+        Z: (own, 0, block, to_z), ZX: (xx, 0, block, to_z),
         A_LO: (own, 0, block, to_p), A_HI: (own, 0, block, to_m),
         B_LO: (zown, 0, block, to_p), B_HI: (zown, 0, block, to_m),
         RA_LO: (xm, 0, first, to_p), RA_HI: (xp, first, second, to_m),
@@ -132,7 +136,7 @@
         S_RA: (xx, 0, block, to_s), S_RB: (zx, 0, block, to_s),
     }
     arrives = {
-        Z: (zown, core, 0, block),
+        Z: (zown, core, 0, block), ZX: (zx, core, 0, block),
         A_LO: (xm, core, 0, block), A_HI: (xp, core, 0, block),
         B_LO: (zm, core, 0, block), B_HI: (zp, core, 0, block),
         RA_LO: (xx, core, 0, first), RA_HI: (xx, core, first, second),
@@ -149,7 +153,34 @@
         c, k, lo, n = arrives[kind]
         remote(kind, t, c, k, to_s, lo, n).wait_recv()
 
+    def open_chunk(t):
+        weight_load(t, 0).wait()
+        weight_load(t, 1).wait()
+        for kind in (A_LO, A_HI, S_OWN):
+            put(kind, t)
+
+    def pass_a(t):
+        for kind, relay, copy in ((A_LO, RA_LO, S_A_LO), (A_HI, RA_HI, S_A_HI)):
+            got(kind, t)
+            put(relay, t)
+            put(copy, t)
+
+    def over_z(t):
+        return t == 3
+
+    def far_sends(t, fn):
+        @pl.when(over_z(t))
+        def _():
+            fn(ZX, t)
+
+        @pl.when(jnp.logical_not(over_z(t)))
+        def _():
+            fn(RB_LO, t)
+            fn(RB_HI, t)
+
+    open_chunk(0)
     put(Z, 0)
+    open_chunk(1)
 
     for c in small_loads[2:]:
         c.wait()
@@ -207,14 +238,6 @@
         group = lane // SMALL
         ext[...] = jnp.where(group == 0, hi, jnp.where(group == 1, mid, lo)).astype(BF16)
 
-    def split_rows(v):
-        n = v.shape[0]
-        gate_row = lax.broadcasted_iota(jnp.int32, (n, LANES), 0) % SMALL < SMALL // 2
-        vf = v.astype(F32)
-        return jnp.concatenate(
-            [jnp.where(gate_row, vf, 0.0), jnp.where(gate_row, 0.0, vf)], axis=1
-        ).astype(BF16)
-
     def start_chunk(t, slot):
         rhs = split_rows(gath[t, own, core, 2 * depth:, :])
         pad = jnp.zeros((LANES - 3 * SMALL, 2 * LANES), BF16)
@@ -239,62 +262,72 @@
         left[:, :n_pop * SMALL] = hi
         left[:, n_pop * SMALL:] = (prod - hi.astype(F32)).astype(BF16)
 
-    def out_copy(t, k):
-        dst = (ug_hbm, uu_hbm)[k]
-        col = pl.multiple_of(t * LANES, LANES)
-        return pltpu.make_async_copy(stage.at[t, k], dst.at[:, pl.ds(col, LANES)], osem.at[k, t])
-
-    def update_chunk(t):
-        right = split_rows(gath[t, :, :, 2 * depth:, :].reshape(n_pop * SMALL, LANES))
-        upd = dot(left[...], jnp.concatenate([right, right], axis=0)) * out_scale
-        stage[t, 0] = upd[:, :LANES]
-        stage[t, 1] = upd[:, LANES:]
-        out_copy(t, 0).start()
-        out_copy(t, 1).start()
-
-    def phase_two(t, slot):
-        got(S_RA, t)
-        add_chip(t, slot, xx)
-        got(S_RB, t)
-        add_chip(t, slot, zx)
-        finish_chunk(t, slot)
+    def factor_out(t):
+        return pltpu.make_async_copy(gath.at[t, :, :, pl.ds(2 * depth, SMALL)], right_hbm.at[t], osem.at[t])
+
+    open_chunk(2)
+    put(Z, 1)
+    pass_a(0)
 
     @pl.loop(0, chunks + 2)
     def _(i):
+        @pl.when(i + 3 < chunks)
+        def _():
+            open_chunk(i + 3)
+
+        @pl.when(i + 1 < chunks)
+        def _():
+            pass_a(i + 1)
+
         @pl.when(i < chunks)
         def _():
-            put(A_LO, i)
-            put(A_HI, i)
-
-            @pl.when(i + 1 < chunks)
+            got(Z, i)
+            for kind in (B_LO, B_HI):
+                put(kind, i)
+
+            @pl.when(i + 2 < chunks)
             def _():
-                put(Z, i + 1)
-            put(S_OWN, i)
-            got(Z, i)
-            put(B_LO, i)
-            put(B_HI, i)
+                put(Z, i + 2)
             put(S_Z, i)
 
         @pl.when((i >= 1) & (i < chunks + 1))
         def _():
             t = i - 1
-            for kind, relay, copy in (
-                (A_LO, RA_LO, S_A_LO), (A_HI, RA_HI, S_A_HI),
-                (B_LO, RB_LO, S_B_LO), (B_HI, RB_HI, S_B_HI),
-            ):
+            for kind in (S_OWN, S_Z, S_A_LO, S_A_HI, S_RA):
                 got(kind, t)
-                put(relay, t)
+            start_chunk(t, t % 2)
+
+            add_chip(t, t % 2, zown)
+
+            @pl.loop(0, RING)
+            def _(j):
+                add_chip(t, t % 2, at(j, 0))
+
+        @pl.when((i >= 1) & (i < chunks + 1))
+        def _():
+            t = i - 1
+            for kind, relay, copy in ((B_LO, RB_LO, S_B_LO), (B_HI, RB_HI, S_B_HI)):
+                got(kind, t)
+
+                @pl.when(jnp.logical_not(over_z(t)))
+                def _():
+                    put(relay, t)
                 put(copy, t)
 
+        @pl.when(i < chunks)
+        def _():
+            got(RA_LO, i)
+            got(RA_HI, i)
+
+            @pl.when(over_z(i))
+            def _():
+                put(ZX, i)
+            put(S_RA, i)
+
         @pl.when(i >= 2)
         def _():
-            t = i - 2
-            got(RA_LO, t)
-            got(RA_HI, t)
-            put(S_RA, t)
-            got(RB_LO, t)
-            got(RB_HI, t)
-            put(S_RB, t)
+            far_sends(i - 2, got)
+            put(S_RB, i - 2)
 
         @pl.when(i == 0)
         def _():
@@ -313,29 +346,26 @@
         @pl.when((i >= 1) & (i < chunks + 1))
         def _():
             t = i - 1
-            for kind in (S_OWN, S_Z, S_A_LO, S_A_HI, S_B_LO, S_B_HI):
-                got(kind, t)
-            start_chunk(t, t % 2)
-
-            @pl.loop(0, 6)
+            got(S_B_LO, t)
+            got(S_B_HI, t)
+
+            @pl.loop(0, 2)
             def _(j):
-                q = j // 2
-                add_chip(t, t % 2, at(q + q // 2, j % 2))
+                add_chip(t, t % 2, at(1 + 2 * j, 1))
 
         @pl.when(i >= 2)
         def _():
-            phase_two(i - 2, i % 2)
-
-        @pl.when(i == 2)
+            got(S_RB, i - 2)
+            add_chip(i - 2, i % 2, zx)
+            finish_chunk(i - 2, i % 2)
+            factor_out(i - 2).start()
+
+        @pl.when(i == chunks - 1)
         def _():
             @pl.loop(1, n_shard)
             def _(d):
                 spread_copy((sh + d) % n_shard, sh).wait_recv()
             build_left()
-
-        @pl.when((i >= 2) & (i < chunks + 1))
-        def _():
-            update_chunk(i - 2)
 
     ones = jnp.ones((8, LANES), F32)
     for m in range(members):
@@ -352,13 +382,16 @@
     def _(d):
         score_copy(sh, (sh + d) % n_shard).start()
 
-    update_chunk(chunks - 1)
+    def sent(kind, t):
+        c, lo, n, target = sends[kind]
+        remote(kind, t, c, core, target, lo, n).wait_send()
 
     @pl.loop(0, chunks)
     def _(t):
         for kind in range(KINDS):
-            c, lo, n, target = sends[kind]
-            remote(kind, t, c, core, target, lo, n).wait_send()
+            if kind not in (ZX, RB_LO, RB_HI):
+                sent(kind, t)
+        far_sends(t, sent)
 
     @pl.when(pop == sh)
     def _():
@@ -382,8 +415,16 @@
 
     @pl.loop(0, chunks)
     def _(t):
-        out_copy(t, 0).wait()
-        out_copy(t, 1).wait()
+        factor_out(t).wait()
+
+
+def finish_kernel(out_scale, score_ref, left, right, sc_ref, ug_ref, uu_ref):
+    sc_ref[...] = score_ref[...]
+    for t in range(right.shape[0]):
+        rows = split_rows(right[t].reshape(left.shape[1] // 2, LANES))
+        upd = dot(left[...], jnp.concatenate([rows, rows], axis=0)) * out_scale
+        ug_ref[:, t * LANES:(t + 1) * LANES] = upd[:, :LANES]
+        uu_ref[:, t * LANES:(t + 1) * LANES] = upd[:, LANES:]
 
 
 def body(n_pop, n_shard, tokens, wg, wu, a_gate, a_up, h_gate, h_up, fitness, readout):
@@ -399,16 +440,16 @@
     dma = pltpu.SemaphoreType.DMA
     anyspec = pl.BlockSpec(memory_space=pl.ANY)
     vspec = pl.BlockSpec(memory_space=pltpu.VMEM)
-    return pl.pallas_call(
-        functools.partial(kernel, noise, out_scale, n_pop, n_shard),
+    score, left, right = pl.pallas_call(
+        functools.partial(kernel, noise, n_pop, n_shard),
         name="generation",
         out_shape=(
             jax.ShapeDtypeStruct((members, tok_count), F32),
-            jax.ShapeDtypeStruct((depth, cols), F32),
-            jax.ShapeDtypeStruct((depth, cols), F32),
+            jax.ShapeDtypeStruct((depth, 2 * n_pop * SMALL), BF16),
+            jax.ShapeDtypeStruct((chunks, chips, CORES, SMALL, LANES), BF16),
         ),
-        in_specs=[anyspec] * 7 + [vspec, vspec],
-        out_specs=(vspec, anyspec, anyspec),
+        in_specs=[anyspec] * 9,
+        out_specs=(vspec, vspec, anyspec),
         scratch_shapes=[
             pltpu.VMEM((rows, width), BF16),
             pltpu.VMEM((chunks, chips, CORES, block, LANES), BF16),
@@ -420,22 +461,33 @@
             pltpu.VMEM((members, ranks, width), BF16),
             pltpu.VMEM((members, ranks, cols), BF16),
             pltpu.VMEM((members, ranks, cols), BF16),
+            pltpu.VMEM((1, members), BF16),
+            pltpu.VMEM((chunks, LANES), F32),
             pltpu.VMEM((n_pop, SMALL, depth + LANES), BF16),
             pltpu.VMEM((n_pop, SMALL, depth + LANES), BF16),
-            pltpu.VMEM((depth, 2 * n_pop * SMALL), BF16),
-            pltpu.VMEM((chunks, 2, depth, LANES), F32),
             pltpu.VMEM((n_shard, members, tok_count), F32),
             dma((KINDS, chunks)), dma((KINDS, chunks)),
-            dma((2, chunks)), dma((6,)),
+            dma((2, chunks)), dma((8,)),
             dma((n_pop,)), dma((1,)),
             dma((n_shard,)), dma((n_shard,)),
             dma((n_shard,)), dma((n_shard,)),
-            dma((2, chunks)),
+            dma((chunks,)),
         ],
         compiler_params=pltpu.CompilerParams(
             collective_id=0, has_side_effects=True, vmem_limit_bytes=56 * 1024 * 1024
         ),
     )(tokens, wg, wu, a_gate, a_up, h_gate, h_up, fitness.reshape(1, members), readout.reshape(chunks, LANES))
+    return pl.pallas_call(
+        functools.partial(finish_kernel, out_scale),
+        name="updates",
+        out_shape=(
+            jax.ShapeDtypeStruct((members, tok_count), F32),
+            jax.ShapeDtypeStruct((depth, cols), F32),
+            jax.ShapeDtypeStruct((depth, cols), F32),
+        ),
+        in_specs=[vspec] * 3,
+        out_specs=(vspec,) * 3,
+    )(score, left, right)
 
 
 def solution(mesh):

time: 105 us -> 92.2 us (0.88); the launches traced: 103 us -> 92.1 us
  Pallas kernels: 97.1 us -> 91.4 us
  local copies, waits for them, and re-layouts: 5.58 us -> 0 us
    pallas_call x1 -> x2, Pallas kernels: 97.1 us -> 91.4 us  [the longest x1 88.5 us: body(): pl.pallas_call(functools.partial(kernel, noise, n_pop, n_shard), name='ge...]
    unnamed x3 -> x0, local copies, waits for them, and re-layouts: 5.58 us -> none
where the time goes in v2:
time: 92.2 us; the launch traced here: 92.1 us
  Pallas kernels  91.4 us (99%)
    pallas_call x1, Pallas kernels, body(): pl.pallas_call(functools.partial(kernel, noise, n_pop, n_shard), name='ge...  88.5 us
    pallas_call x1, Pallas kernels, body(): pl.pallas_call(functools.partial(finish_kernel, out_scale), name='updates...  2.97 us

profile of v2, /device:TPU:1, one launch (start us, length us, event | category | flops | bytes accessed | tf_op | source)
XLA Modules:
  0.0 92.1 jit_solution(3030435990777990955)
XLA Ops:
  0.6 88.5 %generation.1 = (f32[2,480]{1,0:T(2,128)}, bf16[256,512]{1,0:T(8,128)(2,1)}, bf16[7,8,2,16,128]{4,3,2,1,0:T(8,128)(2,1)}) custom-call(bf16[2,480,4096]{2,1,0:T(8,128)(2,1)} %tok_hbm.1, bf16[256,896]{1,0:T(8,128)(2,1)} %wg_hbm.1, bf16[256,896]{1,0:T(8,128)(2,1)} %wu_hbm.1, bf16[2,4,4096]{2,1,0:T(4,128)(2,1)} %ag_hbm.1, bf16[2,4,4096]{2,1,0:T(4,128)(2,1)} %au_hbm.1, ...), custom_call_target="tpu_custom_call" | custom-call | tf_op jit(solution)/shard_map/generation/pallas_call | solution.py:443
  89.1 3.0 %updates.1 = (f32[2,480]{1,0:T(2,128)}, f32[256,896]{1,0:T(8,128)}, f32[256,896]{1,0:T(8,128)}) custom-call(f32[2,480]{1,0:T(2,128)} %get-tuple-element.6.score_ref, bf16[256,512]{1,0:T(8,128)(2,1)} %get-tuple-element.7.left, bf16[7,8,2,16,128]{4,3,2,1,0:T(8,128)(2,1)} %get-tuple-element.8.right), custom_call_target="tpu_custom_call" | custom-call | tf_op jit(solution)/shard_map/updates/pallas_call | solution.py:480

commit v3 on v2

v3 whole, which is shorter than its diff:
```python
import functools
import math

import jax
import jax.numpy as jnp
from jax import lax
from jax.experimental import pallas as pl
from jax.experimental.pallas import tpu as pltpu
from jax.sharding import PartitionSpec as P

MESH = pl.DeviceIdType.MESH
F32 = jnp.float32
BF16 = jnp.bfloat16
LANES = 128
RING = 4
CORES = 2
SMALL = 16
(Z, A_LO, A_HI, B_LO, B_HI, RA_LO, RA_HI, RB_LO, RB_HI,
 S_OWN, S_Z, S_A_LO, S_A_HI, S_B_LO, S_B_HI, S_RA, S_RB) = range(17)
BLOCKS = 15
W_Z, W_A_LO, W_A_HI, W_B_LO, W_B_HI, W_RA, W_RB, W_S_FIRST, W_S_B, W_S_RB = range(10)
WAITS = 10
BRINGS = {W_S_FIRST: 5, W_S_B: 2}
LANDS = {
    Z: W_Z, A_LO: W_A_LO, A_HI: W_A_HI, B_LO: W_B_LO, B_HI: W_B_HI,
    RA_LO: W_RA, RA_HI: W_RA, RB_LO: W_RB, RB_HI: W_RB,
    S_OWN: W_S_FIRST, S_Z: W_S_FIRST, S_A_LO: W_S_FIRST, S_A_HI: W_S_FIRST, S_RA: W_S_FIRST,
    S_B_LO: W_S_B, S_B_HI: W_S_B, S_RB: W_S_RB,
}


def dot(a, b, dims=((1,), (0,)), precision=None):
    return lax.dot_general(a, b, (dims, ((), ())), precision=precision, preferred_element_type=F32)


def three_terms(v):
    hi = v.astype(BF16)
    rest = v - hi.astype(F32)
    mid = rest.astype(BF16)
    return hi, mid, (rest - mid.astype(F32)).astype(BF16)


def by_kind(v, n):
    v = v.astype(F32).reshape(n, SMALL, v.shape[-1])
    half = SMALL // 2
    return [v[:, k * half:(k + 1) * half].reshape(n * half, v.shape[-1]) for k in range(2)]


def split_rows(v):
    n = v.shape[0]
    gate_row = lax.broadcasted_iota(jnp.int32, (n, LANES), 0) % SMALL < SMALL // 2
    vf = v.astype(F32)
    return jnp.concatenate(
        [jnp.where(gate_row, vf, 0.0), jnp.where(gate_row, 0.0, vf)], axis=1
    ).astype(BF16)


def kernel(
    noise, n_pop, n_shard,
    tok_hbm, wg_hbm, wu_hbm, ag_hbm, au_hbm, hg_hbm, hu_hbm, fit_hbm, ro_hbm,
    sc_ref, left_hbm, right_hbm,
    tok, gath, acc, total, ext, fac, ag, au, hg, hu, fit_ref, ro_ref, msg, abuf, left, parts,
    send, recv, wsem, lsem, asend, arecv, bsend, brecv, psend, precv, osem,
):
    pop, sh = lax.axis_index("pop"), lax.axis_index("shard")
    core, chip = pop % CORES, pop // CORES
    x, zh = chip % RING, chip // RING
    chunks = recv.shape[1]
    chips = n_pop // CORES
    depth = wg_hbm.shape[0]
    rows = tok.shape[0]
    members = tok_hbm.shape[0]
    per_member = rows // members
    block = 2 * depth + SMALL
    first = depth + SMALL
    span = CORES * depth

    def at(dx, dz):
        return (zh + dz) % 2 * RING + (x + dx) % RING

    def place(t, c, k=0):
        return (t * chips + c) * CORES + k

    def dev(c, k):
        return (c * CORES + k, sh)

    own, zown = at(0, 0), at(0, 1)
    xp, xm, xx = at(1, 0), at(3, 0), at(2, 0)
    zp, zm, zx = at(1, 1), at(3, 1), at(2, 1)

    def weight_load(t, k):
        src = (wg_hbm, wu_hbm)[k]
        col = pl.multiple_of(t * LANES, LANES)
        return pltpu.make_async_copy(
            src.at[:, pl.ds(col, LANES)],
            gath.at[place(t, own, core), pl.ds(k * depth, depth)], wsem.at[t],
        )

    small_loads = [
        pltpu.make_async_copy(a, b, lsem.at[i])
        for i, (a, b) in enumerate(((hg_hbm, hg), (hu_hbm, hu), (ag_hbm, ag), (au_hbm, au), (fit_hbm, fit_ref), (ro_hbm, ro_ref)))
    ]
    tok_loads = [
        pltpu.make_async_copy(
            tok_hbm.at[m], tok.at[pl.ds(m * per_member, per_member)], lsem.at[6 + m]
        )
        for m in range(members)
    ]
    for c in small_loads[:2]:
        c.start()

    @pl.loop(0, chunks)
    def _(t):
        weight_load(t, 0).start()
        weight_load(t, 1).start()

    for c in small_loads[2:] + tok_loads:
        c.start()

    barrier = pltpu.get_barrier_semaphore()

    @pl.loop(1, n_pop)
    def _(d):
        pl.semaphore_signal(barrier, inc=1, device_id=((pop + d) % n_pop, sh), device_id_type=MESH)

    @pl.loop(1, n_shard)
    def _(d):
        pl.semaphore_signal(barrier, inc=1, device_id=(pop, (sh + d) % n_shard), device_id_type=MESH)

    for c in small_loads[:2]:
        c.wait()

    def pack(gate, up):
        return jnp.concatenate(
            [gate[0].astype(F32), gate[1].astype(F32), up[0].astype(F32), up[1].astype(F32)], axis=0
        ).astype(BF16)

    factors = pack(hg, hu)
    for t in range(chunks):
        gath[place(t, own, core), 2 * depth:, :] = factors[:, t * LANES:(t + 1) * LANES]

    pl.semaphore_wait(barrier, n_pop - 1 + n_shard - 1)

    def remote(kind, t, c, target, lo=0, n=block):
        ref = gath.at[place(t, c, core), pl.ds(lo, n)]
        return pltpu.make_async_remote_copy(
            src_ref=ref, dst_ref=ref, send_sem=send.at[0], recv_sem=recv.at[LANDS[kind], t],
            device_id=target, device_id_type=MESH,
        )

    to_z, to_p, to_m, to_s = dev(zown, core), dev(xp, core), dev(xm, core), dev(own, 1 - core)
    second = block - first

    sends = {
        Z: (own, 0, block, to_z),
        A_LO: (own, 0, block, to_p), A_HI: (own, 0, block, to_m),
        B_LO: (zown, 0, block, to_p), B_HI: (zown, 0, block, to_m),
        RA_LO: (xm, 0, first, to_p), RA_HI: (xp, first, second, to_m),
        RB_LO: (zm, first, second, to_p), RB_HI: (zp, 0, first, to_m),
        S_OWN: (own, 0, block, to_s), S_Z: (zown, 0, block, to_s),
        S_A_LO: (xm, 0, block, to_s), S_A_HI: (xp, 0, block, to_s),
        S_B_LO: (zm, 0, block, to_s), S_B_HI: (zp, 0, block, to_s),
        S_RA: (xx, 0, block, to_s), S_RB: (zx, 0, block, to_s),
    }
    def put(kind, t):
        c, lo, n, target = sends[kind]
        remote(kind, t, c, target, lo, n).start()

    def bulk(ref, send_sem, recv_sem):
        return pltpu.make_async_remote_copy(
            src_ref=ref, dst_ref=ref, send_sem=send_sem, recv_sem=recv_sem,
            device_id=to_s, device_id_type=MESH,
        )

    def got(what, t):
        bulk(gath.at[pl.ds(0, BRINGS.get(what, 1))], send.at[0], recv.at[what, t]).wait_recv()

    def open_chunk(t):
        both = gath.at[0, pl.ds(0, 2 * depth)]
        pltpu.make_async_copy(both, both, wsem.at[t]).wait()
        for kind in (A_LO, A_HI, S_OWN):
            put(kind, t)

    def pass_a(t):
        for what, relay, copy in ((W_A_LO, RA_LO, S_A_LO), (W_A_HI, RA_HI, S_A_HI)):
            got(what, t)
            put(relay, t)
            put(copy, t)

    open_chunk(0)
    put(Z, 0)
    open_chunk(1)

    for c in small_loads[2:]:
        c.wait()
    rank_rows = pack(ag, au)
    for k in range(3):
        fac[k * SMALL:(k + 1) * SMALL, :] = rank_rows
    fac[3 * SMALL:, :] = jnp.zeros((LANES - 3 * SMALL, fac.shape[1]), BF16)
    fit = fit_ref[...].astype(F32)
    row16 = lax.broadcasted_iota(jnp.int32, (SMALL, LANES), 0)
    f0 = jnp.broadcast_to(fit[:, 0:1], (SMALL, LANES))
    f1 = jnp.broadcast_to(fit[:, 1:2], (SMALL, LANES))
    fit_rows = jnp.where(row16 // 4 % 2 == 0, f0, f1).astype(BF16)
    for q in range(n_pop):
        msg[q, :, :depth] = rank_rows[:, q * depth:(q + 1) * depth]
        msg[q, :, depth:] = fit_rows

    def factor_copy(q):
        return pltpu.make_async_remote_copy(
            src_ref=msg.at[q], dst_ref=abuf.at[sh], send_sem=asend.at[0], recv_sem=arecv.at[0],
            device_id=(q, sh), device_id_type=MESH,
        )

    def spread_copy(target):
        return pltpu.make_async_remote_copy(
            src_ref=abuf.at[sh], dst_ref=abuf.at[sh], send_sem=bsend.at[0], recv_sem=brecv.at[0],
            device_id=(pop, target), device_id_type=MESH,
        )

    others = pl.ds(0, n_shard - 1)
    spread_all = bulk(abuf.at[others], bsend.at[0], brecv.at[0])

    @pl.when(pop == sh)
    def _():
        @pl.loop(1, n_pop)
        def _(d):
            factor_copy((pop + d) % n_pop).start()
        abuf[pop] = msg[pop]

    total[...] = jnp.zeros_like(total)

    def project():
        for c in tok_loads:
            c.wait()
        acc[0, :, :LANES] = jnp.zeros((rows, LANES), F32)

        @pl.loop(0, tok.shape[1] // span)
        def _(k):
            cols = pl.ds(pl.multiple_of(k * span, span), span)
            acc[0, :, :LANES] += dot(tok[:, cols], fac[:, cols], ((1,), (1,)))

        row = lax.broadcasted_iota(jnp.int32, (rows, LANES), 0)
        lane = lax.broadcasted_iota(jnp.int32, (rows, LANES), 1)
        mine = (row // per_member) == (lane // 4 % 2)
        p = jnp.where(mine, acc[0, :, :LANES] * noise, 0.0)
        hi, mid, lo = (v.astype(F32) for v in three_terms(p))
        group = lane // SMALL
        ext[...] = jnp.where(group == 0, hi, jnp.where(group == 1, mid, lo)).astype(BF16)

    def start_chunk(t, slot):
        rhs = split_rows(gath[place(t, own, core), 2 * depth:, :])
        pad = jnp.zeros((LANES - 3 * SMALL, 2 * LANES), BF16)
        acc[slot] = dot(ext[...], jnp.concatenate([rhs, rhs, rhs, pad], axis=0))

    def add_chip(t, slot, c):
        cols = pl.ds(pl.multiple_of(c * span, span), span)
        both = pl.ds(place(t, c), CORES)
        gate = gath[both, :depth, :].reshape(span, LANES)
        up = gath[both, depth:2 * depth, :].reshape(span, LANES)
        acc[slot] += dot(tok[:, cols], jnp.concatenate([gate, up], axis=1))

    def finish_chunk(t, slot):
        gate, up = acc[slot, :, :LANES], acc[slot, :, LANES:]
        hidden = gate / (1.0 + jnp.exp(-gate)) * up
        total[...] += hidden * ro_ref[pl.ds(t, 1), :]

    def build_left():
        a = abuf[:, :, :depth].reshape(n_pop * SMALL, depth).astype(F32)
        f = abuf[:, :, depth:].reshape(n_pop * SMALL, LANES).astype(F32)
        prod = a * jnp.concatenate([f] * (depth // LANES), axis=1)
        for k, part in enumerate(by_kind(prod, n_pop)):
            part = part.T
            hi = part.astype(BF16)
            n = part.shape[1]
            left[k, :, :n] = hi
            left[k, :, n:] = (part - hi.astype(F32)).astype(BF16)

    def left_out():
        return pltpu.make_async_copy(left, left_hbm, osem.at[1])

    def factor_out(t):
        return pltpu.make_async_copy(
            gath.at[pl.ds(place(t, 0), n_pop), pl.ds(2 * depth, SMALL)], right_hbm.at[t], osem.at[0]
        )

    open_chunk(2)
    put(Z, 1)
    pass_a(0)

    @pl.loop(0, chunks + 2)
    def _(i):
        @pl.when(i + 3 < chunks)
        def _():
            open_chunk(i + 3)

        @pl.when(i + 1 < chunks)
        def _():
            pass_a(i + 1)

        @pl.when(i < chunks)
        def _():
            got(W_Z, i)
            for kind in (B_LO, B_HI):
                put(kind, i)

            @pl.when(i + 2 < chunks)
            def _():
                put(Z, i + 2)
            put(S_Z, i)

        @pl.when((i >= 1) & (i < chunks + 1))
        def _():
            t = i - 1
            for what, relay, copy in ((W_B_LO, RB_LO, S_B_LO), (W_B_HI, RB_HI, S_B_HI)):
                got(what, t)
                put(relay, t)
                put(copy, t)

        @pl.when((i >= 1) & (i < chunks + 1))
        def _():
            t = i - 1
            got(W_S_FIRST, t)
            start_chunk(t, t % 2)

            add_chip(t, t % 2, zown)

            @pl.loop(0, RING)
            def _(j):
                add_chip(t, t % 2, at(j, 0))

        @pl.when(i < chunks)
        def _():
            got(W_RA, i)
            put(S_RA, i)

        @pl.when(i >= 2)
        def _():
            got(W_RB, i - 2)
            put(S_RB, i - 2)

        @pl.when(i == 0)
        def _():
            project()

        @pl.when(i == 1)
        def _():
            @pl.when(pop != sh)
            def _():
                factor_copy(pop).wait_recv()

            @pl.loop(1, n_shard)
            def _(d):
                spread_copy((sh + d) % n_shard).start()

        @pl.when((i >= 1) & (i < chunks + 1))
        def _():
            t = i - 1
            got(W_S_B, t)

            @pl.loop(0, 2)
            def _(j):
                add_chip(t, t % 2, at(1 + 2 * j, 1))

        @pl.when(i >= 2)
        def _():
            got(W_S_RB, i - 2)
            add_chip(i - 2, i % 2, zx)
            finish_chunk(i - 2, i % 2)
            factor_out(i - 2).start()

        @pl.when(i == chunks - 1)
        def _():
            spread_all.wait_recv()
            build_left()
            left_out().start()

    ones = jnp.ones((SMALL, 3 * LANES), BF16)
    for m in range(members):
        part = dot(ones, jnp.concatenate(three_terms(total[m * per_member:(m + 1) * per_member, :]), axis=1), ((1,), (1,)))
        parts[sh, m:m + 1, :] = part[0:1, :]

    def score_copy(target):
        return pltpu.make_async_remote_copy(
            src_ref=parts.at[sh], dst_ref=parts.at[sh], send_sem=psend.at[0], recv_sem=precv.at[0],
            device_id=(pop, target), device_id_type=MESH,
        )

    @pl.loop(1, n_shard)
    def _(d):
        score_copy((sh + d) % n_shard).start()

    bulk(gath.at[pl.ds(0, chunks * BLOCKS)], send.at[0], recv.at[0, 0]).wait_send()

    @pl.when(pop == sh)
    def _():
        bulk(msg.at[others], asend.at[0], arecv.at[0]).wait_send()

    spread_all.wait_send()
    pltpu.make_async_copy(right_hbm, right_hbm, osem.at[0]).wait()
    left_out().wait()
    score_all = bulk(parts.at[others], psend.at[0], precv.at[0])
    score_all.wait_send()
    score_all.wait_recv()

    score = parts[0]
    for s in range(1, n_shard):
        score = score + parts[s]
    sc_ref[...] = score


def finish_kernel(out_scale, score_ref, left, right, sc_ref, ug_ref, uu_ref):
    sc_ref[...] = score_ref[...]
    chunks, n = right.shape[0], left.shape[2] // SMALL
    for t in range(0, chunks, 2):
        pair = [by_kind(right[u].reshape(n * SMALL, LANES), n) for u in range(t, min(t + 2, chunks))]
        for k, out in enumerate((ug_ref, uu_ref)):
            rows = jnp.concatenate([p[k].astype(BF16) for p in pair], axis=1)
            out[:, t * LANES:t * LANES + rows.shape[1]] = (
                dot(left[k], jnp.concatenate([rows, rows], axis=0)) * out_scale
            )


def body(n_pop, n_shard, tokens, wg, wu, a_gate, a_up, h_gate, h_up, fitness, readout):
    members, tok_count, width = tokens.shape
    depth, cols = wg.shape
    ranks = a_gate.shape[1]
    chunks = cols // LANES
    rows = members * tok_count
    noise = 0.25 / math.sqrt(width * ranks)
    out_scale = 1.0 / math.sqrt(n_pop * members * ranks)
    block = 2 * depth + SMALL
    dma = pltpu.SemaphoreType.DMA
    anyspec = pl.BlockSpec(memory_space=pl.ANY)
    vspec = pl.BlockSpec(memory_space=pltpu.VMEM)
    score, left, right = pl.pallas_call(
        functools.partial(kernel, noise, n_pop, n_shard),
        name="generation",
        out_shape=(
            jax.ShapeDtypeStruct((members, tok_count), F32),
            jax.ShapeDtypeStruct((2, depth, n_pop * SMALL), BF16),
            jax.ShapeDtypeStruct((chunks, n_pop, SMALL, LANES), BF16),
        ),
        in_specs=[anyspec] * 9,
        out_specs=(vspec, anyspec, anyspec),
        scratch_shapes=[
            pltpu.VMEM((rows, width), BF16),
            pltpu.VMEM((chunks * n_pop, block, LANES), BF16),
            pltpu.VMEM((2, rows, 2 * LANES), F32),
            pltpu.VMEM((rows, LANES), F32),
            pltpu.VMEM((rows, LANES), BF16),
            pltpu.VMEM((LANES, width), BF16),
            pltpu.VMEM((members, ranks, width), BF16),
            pltpu.VMEM((members, ranks, width), BF16),
            pltpu.VMEM((members, ranks, cols), BF16),
            pltpu.VMEM((members, ranks, cols), BF16),
            pltpu.VMEM((1, members), BF16),
            pltpu.VMEM((chunks, LANES), F32),
            pltpu.VMEM((n_pop, SMALL, depth + LANES), BF16),
            pltpu.VMEM((n_pop, SMALL, depth + LANES), BF16),
            pltpu.VMEM((2, depth, n_pop * SMALL), BF16),
            pltpu.VMEM((n_shard, members, tok_count), F32),
            dma((1,)), dma((WAITS, chunks)),
            dma((chunks,)), dma((8,)),
            dma((1,)), dma((1,)), dma((1,)), dma((1,)), dma((1,)), dma((1,)),
            dma((2,)),
        ],
        compiler_params=pltpu.CompilerParams(
            collective_id=0, has_side_effects=True, vmem_limit_bytes=56 * 1024 * 1024
        ),
    )(tokens, wg, wu, a_gate, a_up, h_gate, h_up, fitness.reshape(1, members), readout.reshape(chunks, LANES))
    return pl.pallas_call(
        functools.partial(finish_kernel, out_scale),
        name="updates",
        out_shape=(
            jax.ShapeDtypeStruct((members, tok_count), F32),
            jax.ShapeDtypeStruct((depth, cols), F32),
            jax.ShapeDtypeStruct((depth, cols), F32),
        ),
        grid=(2,),
        in_specs=[
            pl.BlockSpec((members, tok_count), lambda i: (0, 0)),
            pl.BlockSpec((2, depth // 2, n_pop * SMALL), lambda i: (0, i, 0)),
            pl.BlockSpec((chunks, n_pop, SMALL, LANES), lambda i: (0, 0, 0, 0)),
        ],
        out_specs=(
            pl.BlockSpec((members, tok_count), lambda i: (0, 0)),
            pl.BlockSpec((depth // 2, cols), lambda i: (i, 0)),
            pl.BlockSpec((depth // 2, cols), lambda i: (i, 0)),
        ),
    )(score, left, right)


def solution(mesh):
    placed = (
        P("pop", None, None),
        P("pop", "shard"),
        P("pop", "shard"),
        P("pop", None, None),
        P("pop", None, None),
        P("pop", None, "shard"),
        P("pop", None, "shard"),
        P("pop"),
        P("shard"),
    )
    return jax.shard_map(
        functools.partial(body, mesh.shape["pop"], mesh.shape["shard"]),
        mesh=mesh,
        in_specs=placed,
        out_specs=(P("pop", None), P("pop", "shard"), P("pop", "shard")),
        check_vma=False,
    )
```

time: 92.2 us -> 88.4 us (0.959)
  Pallas kernels: 91.4 us -> 87.6 us
    pallas_call x1, Pallas kernels: 88.5 us -> 84.9 us  [body(): pl.pallas_call(functools.partial(kernel, noise, n_pop, n_shard), name='ge...]
where the time goes in v3:
time: 88.4 us; the launch traced here: 88.3 us
  Pallas kernels  87.6 us (99%)
    pallas_call x1, Pallas kernels, body(): pl.pallas_call(functools.partial(kernel, noise, n_pop, n_shard), name='ge...  84.9 us
    pallas_call x1, Pallas kernels, body(): pl.pallas_call(functools.partial(finish_kernel, out_scale), name='updates...  2.68 us

profile of v3, /device:TPU:1, one launch (start us, length us, event | category | flops | bytes accessed | tf_op | source)
XLA Modules:
  0.0 88.3 jit_solution(14330489884929038909)
XLA Ops:
  0.6 84.9 %generation.1 = (f32[2,480]{1,0:T(2,128)}, bf16[2,256,256]{2,1,0:T(8,128)(2,1)}, bf16[7,16,16,128]{3,2,1,0:T(8,128)(2,1)}) custom-call(bf16[2,480,4096]{2,1,0:T(8,128)(2,1)} %tok_hbm.1, bf16[256,896]{1,0:T(8,128)(2,1)} %wg_hbm.1, bf16[256,896]{1,0:T(8,128)(2,1)} %wu_hbm.1, bf16[2,4,4096]{2,1,0:T(4,128)(2,1)} %ag_hbm.1, bf16[2,4,4096]{2,1,0:T(4,128)(2,1)} %au_hbm.1, ...), custom_call_target="tpu_custom_call" | custom-call | tf_op jit(solution)/shard_map/generation/pallas_call | solution.py:436
  85.6 2.7 %updates.1 = (f32[2,480]{1,0:T(2,128)}, f32[256,896]{1,0:T(8,128)}, f32[256,896]{1,0:T(8,128)}) custom-call(f32[2,480]{1,0:T(2,128)} %get-tuple-element.6.score_ref, bf16[2,256,256]{2,1,0:T(8,128)(2,1)} %get-tuple-element.7.left, bf16[7,16,16,128]{3,2,1,0:T(8,128)(2,1)} %get-tuple-element.8.right), custom_call_target="tpu_custom_call" | custom-call | tf_op jit(solution)/shard_map/updates/pallas_call | solution.py:472

commit v4 on v3

--- a/solution.py
+++ b/solution.py
@@ -59,20 +59,21 @@
     noise, n_pop, n_shard,
     tok_hbm, wg_hbm, wu_hbm, ag_hbm, au_hbm, hg_hbm, hu_hbm, fit_hbm, ro_hbm,
     sc_ref, left_hbm, right_hbm,
-    tok, gath, acc, total, ext, fac, ag, au, hg, hu, fit_ref, ro_ref, msg, abuf, left, parts,
-    send, recv, wsem, lsem, asend, arecv, bsend, brecv, psend, precv, osem,
+    tok, gath, hid, acc, total, ext, fac, ag, au, hg, hu, fit_ref, ro_ref, msg, abuf, left, parts,
+    send, hsend, recv, wsem, lsem, asend, arecv, bsend, brecv, psend, precv, osem,
 ):
     pop, sh = lax.axis_index("pop"), lax.axis_index("shard")
     core, chip = pop % CORES, pop // CORES
     x, zh = chip % RING, chip // RING
-    chunks = recv.shape[1]
+    chunks = recv.shape[1] - 1
     chips = n_pop // CORES
     depth = wg_hbm.shape[0]
     rows = tok.shape[0]
     members = tok_hbm.shape[0]
     per_member = rows // members
-    block = 2 * depth + SMALL
-    first = depth + SMALL
+    block = 2 * depth
+    cols = chunks * LANES
+    half_cols = cols // 2 // LANES * LANES + LANES
     span = CORES * depth
 
     def at(dx, dz):
@@ -135,9 +136,7 @@
             [gate[0].astype(F32), gate[1].astype(F32), up[0].astype(F32), up[1].astype(F32)], axis=0
         ).astype(BF16)
 
-    factors = pack(hg, hu)
-    for t in range(chunks):
-        gath[place(t, own, core), 2 * depth:, :] = factors[:, t * LANES:(t + 1) * LANES]
+    hid[place(0, own, core)] = pack(hg, hu)
 
     pl.semaphore_wait(barrier, n_pop - 1 + n_shard - 1)
 
@@ -149,14 +148,13 @@
         )
 
     to_z, to_p, to_m, to_s = dev(zown, core), dev(xp, core), dev(xm, core), dev(own, 1 - core)
-    second = block - first
 
     sends = {
         Z: (own, 0, block, to_z),
         A_LO: (own, 0, block, to_p), A_HI: (own, 0, block, to_m),
         B_LO: (zown, 0, block, to_p), B_HI: (zown, 0, block, to_m),
-        RA_LO: (xm, 0, first, to_p), RA_HI: (xp, first, second, to_m),
-        RB_LO: (zm, first, second, to_p), RB_HI: (zp, 0, first, to_m),
+        RA_LO: (xm, 0, depth, to_p), RA_HI: (xp, depth, depth, to_m),
+        RB_LO: (zm, depth, depth, to_p), RB_HI: (zp, 0, depth, to_m),
         S_OWN: (own, 0, block, to_s), S_Z: (zown, 0, block, to_s),
         S_A_LO: (xm, 0, block, to_s), S_A_HI: (xp, 0, block, to_s),
         S_B_LO: (zm, 0, block, to_s), S_B_HI: (zp, 0, block, to_s),
@@ -165,6 +163,18 @@
     def put(kind, t):
         c, lo, n, target = sends[kind]
         remote(kind, t, c, target, lo, n).start()
+
+    def put_factors(kind):
+        c, lo, n, target = sends[kind]
+        width = pl.ds(0, cols) if n == block else pl.ds(0, half_cols) if lo == 0 else pl.ds(half_cols, cols - half_cols)
+        ref = hid.at[place(0, c, core), :, width]
+        pltpu.make_async_remote_copy(
+            src_ref=ref, dst_ref=ref, send_sem=hsend.at[0], recv_sem=recv.at[LANDS[kind], chunks],
+            device_id=target, device_id_type=MESH,
+        ).start()
+
+    def got_factors(what):
+        bulk(hid.at[pl.ds(0, BRINGS.get(what, 1))], hsend.at[0], recv.at[what, chunks]).wait_recv()
 
     def bulk(ref, send_sem, recv_sem):
         return pltpu.make_async_remote_copy(
@@ -249,7 +259,7 @@
         ext[...] = jnp.where(group == 0, hi, jnp.where(group == 1, mid, lo)).astype(BF16)
 
     def start_chunk(t, slot):
-        rhs = split_rows(gath[place(t, own, core), 2 * depth:, :])
+        rhs = split_rows(hid[place(0, own, core), :, pl.ds(pl.multiple_of(t * LANES, LANES), LANES)])
         pad = jnp.zeros((LANES - 3 * SMALL, 2 * LANES), BF16)
         acc[slot] = dot(ext[...], jnp.concatenate([rhs, rhs, rhs, pad], axis=0))
 
@@ -279,10 +289,8 @@
     def left_out():
         return pltpu.make_async_copy(left, left_hbm, osem.at[1])
 
-    def factor_out(t):
-        return pltpu.make_async_copy(
-            gath.at[pl.ds(place(t, 0), n_pop), pl.ds(2 * depth, SMALL)], right_hbm.at[t], osem.at[0]
-        )
+    def factor_out():
+        return pltpu.make_async_copy(hid, right_hbm, osem.at[0])
 
     open_chunk(2)
     put(Z, 1)
@@ -308,6 +316,15 @@
             def _():
                 put(Z, i + 2)
             put(S_Z, i)
+
+        @pl.when(i == chunks - 2)
+        def _():
+            put_factors(Z)
+
+        @pl.when(i == chunks - 1)
+        def _():
+            for kind in (A_LO, A_HI, S_OWN):
+                put_factors(kind)
 
         @pl.when((i >= 1) & (i < chunks + 1))
         def _():
@@ -317,6 +334,16 @@
                 put(relay, t)
                 put(copy, t)
 
+        @pl.when(i == chunks)
+        def _():
+            got_factors(W_Z)
+            for kind in (B_LO, B_HI, S_Z):
+                put_factors(kind)
+            for what, relay, copy in ((W_A_LO, RA_LO, S_A_LO), (W_A_HI, RA_HI, S_A_HI)):
+                got_factors(what)
+                put_factors(relay)
+                put_factors(copy)
+
         @pl.when((i >= 1) & (i < chunks + 1))
         def _():
             t = i - 1
@@ -339,6 +366,15 @@
             got(W_RB, i - 2)
             put(S_RB, i - 2)
 
+        @pl.when(i == chunks + 1)
+        def _():
+            for what, relay, copy in ((W_B_LO, RB_LO, S_B_LO), (W_B_HI, RB_HI, S_B_HI)):
+                got_factors(what)
+                put_factors(relay)
+                put_factors(copy)
+            got_factors(W_RA)
+            put_factors(S_RA)
+
         @pl.when(i == 0)
         def _():
             project()
@@ -367,7 +403,6 @@
             got(W_S_RB, i - 2)
             add_chip(i - 2, i % 2, zx)
             finish_chunk(i - 2, i % 2)
-            factor_out(i - 2).start()
 
         @pl.when(i == chunks - 1)
         def _():
@@ -390,14 +425,19 @@
     def _(d):
         score_copy((sh + d) % n_shard).start()
 
+    got_factors(W_RB)
+    put_factors(S_RB)
     bulk(gath.at[pl.ds(0, chunks * BLOCKS)], send.at[0], recv.at[0, 0]).wait_send()
+    for what in (W_S_FIRST, W_S_B, W_S_RB):
+        got_factors(what)
+    factor_out().start()
+    bulk(hid.at[pl.ds(0, BLOCKS)], hsend.at[0], recv.at[0, 0]).wait_send()
 
     @pl.when(pop == sh)
     def _():
         bulk(msg.at[others], asend.at[0], arecv.at[0]).wait_send()
 
     spread_all.wait_send()
-    pltpu.make_async_copy(right_hbm, right_hbm, osem.at[0]).wait()
     left_out().wait()
     score_all = bulk(parts.at[others], psend.at[0], precv.at[0])
     score_all.wait_send()
@@ -407,18 +447,16 @@
     for s in range(1, n_shard):
         score = score + parts[s]
     sc_ref[...] = score
+    factor_out().wait()
 
 
 def finish_kernel(out_scale, score_ref, left, right, sc_ref, ug_ref, uu_ref):
     sc_ref[...] = score_ref[...]
-    chunks, n = right.shape[0], left.shape[2] // SMALL
-    for t in range(0, chunks, 2):
-        pair = [by_kind(right[u].reshape(n * SMALL, LANES), n) for u in range(t, min(t + 2, chunks))]
-        for k, out in enumerate((ug_ref, uu_ref)):
-            rows = jnp.concatenate([p[k].astype(BF16) for p in pair], axis=1)
-            out[:, t * LANES:t * LANES + rows.shape[1]] = (
-                dot(left[k], jnp.concatenate([rows, rows], axis=0)) * out_scale
-            )
+    n = right.shape[0]
+    rows = by_kind(right[...].reshape(n * SMALL, right.shape[2]), n)
+    for k, out in enumerate((ug_ref, uu_ref)):
+        r = rows[k].astype(BF16)
+        out[...] = dot(left[k], jnp.concatenate([r, r], axis=0)) * out_scale
 
 
 def body(n_pop, n_shard, tokens, wg, wu, a_gate, a_up, h_gate, h_up, fitness, readout):
@@ -429,7 +467,7 @@
     rows = members * tok_count
     noise = 0.25 / math.sqrt(width * ranks)
     out_scale = 1.0 / math.sqrt(n_pop * members * ranks)
-    block = 2 * depth + SMALL
+    block = 2 * depth
     dma = pltpu.SemaphoreType.DMA
     anyspec = pl.BlockSpec(memory_space=pl.ANY)
     vspec = pl.BlockSpec(memory_space=pltpu.VMEM)
@@ -439,13 +477,14 @@
         out_shape=(
             jax.ShapeDtypeStruct((members, tok_count), F32),
             jax.ShapeDtypeStruct((2, depth, n_pop * SMALL), BF16),
-            jax.ShapeDtypeStruct((chunks, n_pop, SMALL, LANES), BF16),
+            jax.ShapeDtypeStruct((n_pop, SMALL, cols), BF16),
         ),
         in_specs=[anyspec] * 9,
         out_specs=(vspec, anyspec, anyspec),
         scratch_shapes=[
             pltpu.VMEM((rows, width), BF16),
             pltpu.VMEM((chunks * n_pop, block, LANES), BF16),
+            pltpu.VMEM((n_pop, SMALL, cols), BF16),
             pltpu.VMEM((2, rows, 2 * LANES), F32),
             pltpu.VMEM((rows, LANES), F32),
             pltpu.VMEM((rows, LANES), BF16),
@@ -460,7 +499,7 @@
             pltpu.VMEM((n_pop, SMALL, depth + LANES), BF16),
             pltpu.VMEM((2, depth, n_pop * SMALL), BF16),
             pltpu.VMEM((n_shard, members, tok_count), F32),
-            dma((1,)), dma((WAITS, chunks)),
+            dma((1,)), dma((1,)), dma((WAITS, chunks + 1)),
             dma((chunks,)), dma((8,)),
             dma((1,)), dma((1,)), dma((1,)), dma((1,)), dma((1,)), dma((1,)),
             dma((2,)),
@@ -481,7 +520,7 @@
         in_specs=[
             pl.BlockSpec((members, tok_count), lambda i: (0, 0)),
             pl.BlockSpec((2, depth // 2, n_pop * SMALL), lambda i: (0, i, 0)),
-            pl.BlockSpec((chunks, n_pop, SMALL, LANES), lambda i: (0, 0, 0, 0)),
+            pl.BlockSpec((n_pop, SMALL, cols), lambda i: (0, 0, 0)),
         ],
         out_specs=(
             pl.BlockSpec((members, tok_count), lambda i: (0, 0)),

time: 88.4 us -> 87.3 us (0.988)
  Pallas kernels: 87.6 us -> 86.5 us
    pallas_call x1, Pallas kernels: 84.9 us -> 83.9 us  [body(): pl.pallas_call(functools.partial(kernel, noise, n_pop, n_shard), name='ge...]
where the time goes in v4:
time: 87.3 us; the launch traced here: 87.1 us
  Pallas kernels  86.5 us (99%)
    pallas_call x1, Pallas kernels, body(): pl.pallas_call(functools.partial(kernel, noise, n_pop, n_shard), name='ge...  83.9 us
    pallas_call x1, Pallas kernels, body(): pl.pallas_call(functools.partial(finish_kernel, out_scale), name='updates...  2.61 us

profile of v4, /device:TPU:1, one launch (start us, length us, event | category | flops | bytes accessed | tf_op | source)
XLA Modules:
  0.0 87.1 jit_solution(5002864555210867706)
XLA Ops:
  0.6 83.9 %generation.1 = (f32[2,480]{1,0:T(2,128)}, bf16[2,256,256]{2,1,0:T(8,128)(2,1)}, bf16[16,16,896]{2,1,0:T(8,128)(2,1)}) custom-call(bf16[2,480,4096]{2,1,0:T(8,128)(2,1)} %tok_hbm.1, bf16[256,896]{1,0:T(8,128)(2,1)} %wg_hbm.1, bf16[256,896]{1,0:T(8,128)(2,1)} %wu_hbm.1, bf16[2,4,4096]{2,1,0:T(4,128)(2,1)} %ag_hbm.1, bf16[2,4,4096]{2,1,0:T(4,128)(2,1)} %au_hbm.1, ...), custom_call_target="tpu_custom_call" | custom-call | tf_op jit(solution)/shard_map/generation/pallas_call | solution.py:474
  84.5 2.6 %updates.1 = (f32[2,480]{1,0:T(2,128)}, f32[256,896]{1,0:T(8,128)}, f32[256,896]{1,0:T(8,128)}) custom-call(f32[2,480]{1,0:T(2,128)} %get-tuple-element.6.score_ref, bf16[2,256,256]{2,1,0:T(8,128)(2,1)} %get-tuple-element.7.left, bf16[16,16,896]{2,1,0:T(8,128)(2,1)} %get-tuple-element.8.right), custom_call_target="tpu_custom_call" | custom-call | tf_op jit(solution)/shard_map/updates/pallas_call | solution.py:511

commit v5 on v4

--- a/solution.py
+++ b/solution.py
@@ -334,6 +334,18 @@
                 put(relay, t)
                 put(copy, t)
 
+        @pl.when((i >= 1) & (i < chunks + 1))
+        def _():
+            t = i - 1
+            got(W_S_FIRST, t)
+            start_chunk(t, t % 2)
+
+            add_chip(t, t % 2, zown)
+
+            @pl.loop(0, RING)
+            def _(j):
+                add_chip(t, t % 2, at(j, 0))
+
         @pl.when(i == chunks)
         def _():
             got_factors(W_Z)
@@ -343,18 +355,6 @@
                 got_factors(what)
                 put_factors(relay)
                 put_factors(copy)
-
-        @pl.when((i >= 1) & (i < chunks + 1))
-        def _():
-            t = i - 1
-            got(W_S_FIRST, t)
-            start_chunk(t, t % 2)
-
-            add_chip(t, t % 2, zown)
-
-            @pl.loop(0, RING)
-            def _(j):
-                add_chip(t, t % 2, at(j, 0))
 
         @pl.when(i < chunks)
         def _():

time: 87.3 us -> 87.2 us (level)
  no operation moved by 1% of the time
where the time goes in v5:
time: 87.2 us; the launch traced here: 87 us
  Pallas kernels  86.4 us (99%)
    pallas_call x1, Pallas kernels, body(): pl.pallas_call(functools.partial(kernel, noise, n_pop, n_shard), name='ge...  83.8 us
    pallas_call x1, Pallas kernels, body(): pl.pallas_call(functools.partial(finish_kernel, out_scale), name='updates...  2.61 us

profile of v5, /device:TPU:1, one launch (start us, length us, event | category | flops | bytes accessed | tf_op | source)
XLA Modules:
  0.0 87.0 jit_solution(16380534330050062376)
XLA Ops:
  0.6 83.8 %generation.1 = (f32[2,480]{1,0:T(2,128)}, bf16[2,256,256]{2,1,0:T(8,128)(2,1)}, bf16[16,16,896]{2,1,0:T(8,128)(2,1)}) custom-call(bf16[2,480,4096]{2,1,0:T(8,128)(2,1)} %tok_hbm.1, bf16[256,896]{1,0:T(8,128)(2,1)} %wg_hbm.1, bf16[256,896]{1,0:T(8,128)(2,1)} %wu_hbm.1, bf16[2,4,4096]{2,1,0:T(4,128)(2,1)} %ag_hbm.1, bf16[2,4,4096]{2,1,0:T(4,128)(2,1)} %au_hbm.1, ...), custom_call_target="tpu_custom_call" | custom-call | tf_op jit(solution)/shard_map/generation/pallas_call | solution.py:474
  84.4 2.6 %updates.1 = (f32[2,480]{1,0:T(2,128)}, f32[256,896]{1,0:T(8,128)}, f32[256,896]{1,0:T(8,128)}) custom-call(f32[2,480]{1,0:T(2,128)} %get-tuple-element.6.score_ref, bf16[2,256,256]{2,1,0:T(8,128)(2,1)} %get-tuple-element.7.left, bf16[16,16,896]{2,1,0:T(8,128)(2,1)} %get-tuple-element.8.right), custom_call_target="tpu_custom_call" | custom-call | tf_op jit(solution)/shard_map/updates/pallas_call | solution.py:511
